TPU v7x, 256 devices: a whole 4x4x8 slice. The times are simulated.
256 devices in a mesh: wide: 32 (over x, z_hi, core), narrow: 8 (over y, z_lo).
Axes of the slice: x: 4, y: 4, z: 8 (z_hi: 4, z_lo: 2; z = z_hi * 2 + z_lo), core: 2. Of those that a mesh axis runs over, the one named last changes fastest.
Arguments:
- initial: float32 [32, 8, 128, 2048], P('wide', 'narrow'), may hold values from -6 to 6
- block_values: bfloat16 [16, 12, 128, 128], replicated, may hold values from -0.0546875 to 0.0546875
- block_index: int32 [16, 12], replicated, may hold values from 0 to 15, as said below
- bond_sites: int32 [12, 2], replicated, may hold values from 0 to 6, as said below
- bond_coupling: float32 [12], replicated, may hold values from -0.25 to 0.25
- pin_sites: int32 [8], replicated, may hold values from 0 to 6
- pin_partner: int32 [8], replicated, may hold values from 0 to 13
- pinned_spins: int32 [14], replicated, may hold values from 0 to 1
- pin_coupling: float32 [8], replicated, may hold values from -0.2 to 0.2
- cross_sites: int32 [4], replicated, may hold values from 0 to 6
- cross_coupling: float32 [4], replicated, may hold values from 0.2 to 0.4
Outputs:
- previous_vector: float32 [32, 8, 128, 2048], P('wide', 'narrow')
- chebyshev_vector: float32 [32, 8, 128, 2048], P('wide', 'narrow')
Inputs may be any that keep to these rules, and one draw needn't show every extreme that they name: `block_index`: each row names 12 different block columns. `bond_sites`: the two spins of a bond differ.
All inputs are finite; a program needn't handle non-finite values.
Results may differ from a plain program's by a relative error of at most 0.0031.
Values may be sent and summed in bfloat16 or wider, within the bound.
A program may use at most 128 MiB of HBM per device.

v0:
```python
import functools

import jax
import jax.numpy as jnp
from jax import lax
from jax.experimental import pallas as pl
from jax.experimental.pallas import tpu as pltpu
from jax.sharding import PartitionSpec as P

MESH = pl.DeviceIdType.MESH
STEPS = 4
CROSS = 4
CHUNK = 256


def bit_at(values, position):
    return jnp.bitwise_and(jnp.right_shift(values, position), 1)


def by_bond(bond, scalars):
    chosen = jnp.full(bond.shape, scalars[0])
    for k in range(1, CROSS):
        chosen = jnp.where(bond == k, scalars[k], chosen)
    return chosen


def packed_column(packed, site, bit):
    low = jnp.bitwise_and(packed, jnp.left_shift(1, site) - 1)
    high = jnp.left_shift(jnp.right_shift(packed, site), site + 1)
    return high | low | jnp.left_shift(bit, site)


def kernel(
    sizes,
    initial,
    block_values,
    block_index,
    bond_sites,
    bond_coupling,
    pin_sites,
    pin_partner,
    pinned_spins,
    pin_coupling,
    cross_sites,
    cross_coupling,
    previous_out,
    current_out,
    values,
    states,
    high,
    low,
    sent,
    received,
    mixer,
    picker,
    load_sem,
    value_sem,
    store_sem,
    send_sem,
    recv_sem,
):
    wide_log, narrow_log, columns, chunks, kept, bonds, pins = sizes
    half = columns // 2
    wide, narrow = lax.axis_index("wide"), lax.axis_index("narrow")
    own_bits = (
        bit_at(wide, wide_log - 1),
        bit_at(wide, 0),
        bit_at(narrow, narrow_log - 1),
        bit_at(narrow, 0),
    )

    def flipped(index, bit, position):
        return index + (1 - 2 * bit) * (1 << position)

    partners = (
        (flipped(wide, own_bits[0], wide_log - 1), narrow),
        (flipped(wide, own_bits[1], 0), narrow),
        (wide, flipped(narrow, own_bits[2], narrow_log - 1)),
        (wide, flipped(narrow, own_bits[3], 0)),
    )

    def load(j):
        return pltpu.make_async_copy(
            initial.at[0, 0, :, pl.ds(pl.multiple_of(j * CHUNK, CHUNK), CHUNK)],
            states.at[1, j],
            load_sem.at[j],
        )

    def load_values(j):
        return pltpu.make_async_copy(
            block_values.at[pl.ds(2 * j, 2)], values.at[pl.ds(2 * j, 2)], value_sem.at[j]
        )

    def exchange(step, j, k):
        rows = pl.ds(k * half, half)
        return pltpu.make_async_remote_copy(
            src_ref=sent.at[step, j, rows],
            dst_ref=received.at[step, j, rows],
            send_sem=send_sem.at[step, j, k],
            recv_sem=recv_sem.at[step, j, k],
            device_id=partners[k],
            device_id_type=MESH,
        )

    def store(out, slot, j):
        return pltpu.make_async_copy(
            states.at[slot, j],
            out.at[0, 0, :, pl.ds(pl.multiple_of(j * CHUNK, CHUNK), CHUNK)],
            store_sem.at[slot - STEPS, j],
        )

    def put(step, j, state):
        rounded = state.astype(jnp.bfloat16)
        packed = jnp.dot(picker[...], rounded, preferred_element_type=jnp.float32)
        sent[step, j] = packed.astype(jnp.bfloat16)
        rest = (state - rounded.astype(jnp.float32)).astype(jnp.bfloat16)
        for part in range(2):
            lanes = slice(part * 128, part * 128 + 128)
            high[step, 2 * j + part] = rounded[:, lanes]
            low[step, 2 * j + part] = rest[:, lanes]
        for k in range(CROSS):
            exchange(step, j, k).start()

    for j in range(chunks):
        load(j).start()
    for j in range(chunks):
        load_values(j).start()
    barrier = pltpu.get_barrier_semaphore()
    for partner in partners:
        pl.semaphore_signal(barrier, inc=1, device_id=partner, device_id_type=MESH)

    sites = [cross_sites[k] for k in range(CROSS)]
    row = lax.broadcasted_iota(jnp.int32, (CROSS * half, columns), 0)
    column = lax.broadcasted_iota(jnp.int32, (CROSS * half, columns), 1)
    bond = row // half
    wanted = packed_column(
        row % half, by_bond(bond, sites), 1 - by_bond(bond, own_bits)
    )
    picker[...] = jnp.where(wanted == column, 1.0, 0.0).astype(jnp.bfloat16)
    pl.semaphore_wait(barrier, CROSS)

    @pl.loop(0, chunks)
    def _(j):
        load(j).wait()
        put(0, j, states[1, j])

    states[0] = jnp.zeros(states.shape[1:], jnp.float32)

    row = lax.broadcasted_iota(jnp.int32, (columns, CROSS * half), 0)
    column = lax.broadcasted_iota(jnp.int32, (columns, CROSS * half), 1)
    bond = column // half
    arriving = packed_column(
        column % half, by_bond(bond, sites), 1 - by_bond(bond, own_bits)
    )
    strength = by_bond(bond, [cross_coupling[k] * 0.5 for k in range(CROSS)])
    crossing = jnp.where(arriving == row, strength, 0.0)
    crossing_high = crossing.astype(jnp.bfloat16)
    crossing_low = (crossing - crossing_high.astype(jnp.float32)).astype(jnp.bfloat16)

    row = lax.broadcasted_iota(jnp.int32, (columns, columns), 0)
    column = lax.broadcasted_iota(jnp.int32, (columns, columns), 1)
    hopping = jnp.zeros((columns, columns), jnp.float32)
    diagonal = jnp.zeros((columns, columns), jnp.float32)
    for b in range(bonds):
        one, two = bond_sites[b, 0], bond_sites[b, 1]
        differ = jnp.bitwise_xor(bit_at(row, one), bit_at(row, two)).astype(jnp.float32)
        target = jnp.bitwise_xor(row, jnp.left_shift(1, one) ^ jnp.left_shift(1, two))
        hopping += jnp.where(target == column, bond_coupling[b] * 0.5 * differ, 0.0)
        diagonal += bond_coupling[b] * 0.25 * (1.0 - 2.0 * differ)
    for p in range(pins):
        aligned = jnp.bitwise_xor(bit_at(row, pin_sites[p]), pinned_spins[pin_partner[p]])
        diagonal += pin_coupling[p] * 0.25 * (1.0 - 2.0 * aligned.astype(jnp.float32))
    for k in range(CROSS):
        parity = jnp.bitwise_xor(bit_at(row, sites[k]), own_bits[k])
        diagonal += cross_coupling[k] * 0.25 * (1.0 - 2.0 * parity.astype(jnp.float32))
    matrix = hopping + jnp.where(row == column, diagonal, 0.0)
    matrix_high = matrix.astype(jnp.bfloat16)
    matrix_low = (matrix - matrix_high.astype(jnp.float32)).astype(jnp.bfloat16)
    mixer[...] = jnp.concatenate(
        [crossing_high, crossing_low, matrix_high, matrix_high, matrix_low], axis=1
    )
    for j in range(chunks):
        load_values(j).wait()

    @pl.loop(0, STEPS)
    def _(step):
        scale = jnp.where(step == 0, 1.0, 2.0)

        @pl.loop(0, chunks)
        def _(j):
            parts = []
            for part in range(2):
                r = 2 * j + part
                gathered = jnp.concatenate(
                    [high[step, block_index[r, q]] for q in range(kept)], axis=1
                )
                blocks = values[r].reshape(kept * 128, 128)
                parts.append(jnp.dot(gathered, blocks, preferred_element_type=jnp.float32))
            total = jnp.concatenate(parts, axis=1)
            own_high = jnp.concatenate([high[step, 2 * j], high[step, 2 * j + 1]], axis=1)
            own_low = jnp.concatenate([low[step, 2 * j], low[step, 2 * j + 1]], axis=1)
            for k in range(CROSS):
                exchange(step, j, k).wait_recv()
            arrived = received[step, j]
            mixed = jnp.concatenate([arrived, arrived, own_high, own_low, own_high], axis=0)
            total += jnp.dot(mixer[...], mixed, preferred_element_type=jnp.float32)
            state = scale * total - states[step, j]
            states[step + 2, j] = state

            @pl.when(step < STEPS - 1)
            def _():
                put(step + 1, j, state)

            @pl.when(step == STEPS - 2)
            def _():
                store(previous_out, STEPS, j).start()

            @pl.when(step == STEPS - 1)
            def _():
                store(current_out, STEPS + 1, j).start()

    @pl.loop(0, STEPS)
    def _(step):
        @pl.loop(0, chunks)
        def _(j):
            for k in range(CROSS):
                exchange(step, j, k).wait_send()

    @pl.loop(0, chunks)
    def _(j):
        store(previous_out, STEPS, j).wait()
        store(current_out, STEPS + 1, j).wait()


def solution(mesh):
    wide_log = mesh.shape["wide"].bit_length() - 1
    narrow_log = mesh.shape["narrow"].bit_length() - 1

    def shards(initial, block_values, block_index, bond_sites, *rest):
        columns, width = initial.shape[2:]
        rows, kept = block_index.shape
        chunks = width // CHUNK
        sizes = (
            wide_log,
            narrow_log,
            columns,
            chunks,
            kept,
            bond_sites.shape[0],
            rest[1].shape[0],
        )
        whole = jax.ShapeDtypeStruct(initial.shape, jnp.float32)
        packed = (STEPS, chunks, CROSS * columns // 2, CHUNK)
        return pl.pallas_call(
            functools.partial(kernel, sizes),
            out_shape=(whole, whole),
            in_specs=[pl.BlockSpec(memory_space=pl.ANY)] * 2
            + [pl.BlockSpec(memory_space=pltpu.SMEM)] * 9,
            out_specs=(pl.BlockSpec(memory_space=pl.ANY),) * 2,
            scratch_shapes=[
                pltpu.VMEM(block_values.shape, jnp.bfloat16),
                pltpu.VMEM((STEPS + 2, chunks, columns, CHUNK), jnp.float32),
                pltpu.VMEM((STEPS, rows, columns, 128), jnp.bfloat16),
                pltpu.VMEM((STEPS, rows, columns, 128), jnp.bfloat16),
                pltpu.VMEM(packed, jnp.bfloat16),
                pltpu.VMEM(packed, jnp.bfloat16),
                pltpu.VMEM((columns, 2 * CROSS * columns // 2 + 3 * columns), jnp.bfloat16),
                pltpu.VMEM((CROSS * columns // 2, columns), jnp.bfloat16),
                pltpu.SemaphoreType.DMA((chunks,)),
                pltpu.SemaphoreType.DMA((chunks,)),
                pltpu.SemaphoreType.DMA((2, chunks)),
                pltpu.SemaphoreType.DMA((STEPS, chunks, CROSS)),
                pltpu.SemaphoreType.DMA((STEPS, chunks, CROSS)),
            ],
            compiler_params=pltpu.CompilerParams(
                collective_id=0, has_side_effects=True, vmem_limit_bytes=48 * 1024 * 1024
            ),
        )(initial, block_values, block_index, bond_sites, *rest)

    slab = P("wide", "narrow", None, None)
    return jax.shard_map(
        shards,
        mesh=mesh,
        in_specs=(slab,) + (P(),) * 10,
        out_specs=(slab, slab),
        check_vma=False,
    )
```

profile of v0, /device:TPU:64, one launch (start us, length us, event | category | flops | bytes accessed | tf_op | source)
XLA Modules:
  0.0 49.8 jit_solution(6280515377084426949)
XLA Ops:
  0.6 0.8 %copy.13.bond_sites = s32[12,2]{1,0:T(8,128)S(1)} copy(s32[12,2]{0,1:T(2,128)} %param.14) | data formatting | bytes 192 | tf_op args[3]
  1.4 0.0 copy-start
  1.4 1.2 %copy-done = f32[1,1,128,2048]{3,2,1,0:T(8,128)S(1)} copy-done((f32[1,1,128,2048]{3,2,1,0:T(8,128)S(1)}, f32[1,1,128,2048]{3,2,1,0:T(8,128)}, u32[]{:S(2)}) %copy-start) | copy-done | bytes 1048600
  2.6 0.0 copy-start.1
  2.6 0.7 %copy-done.1 = s32[16,12]{1,0:T(8,128)S(1)} copy-done((s32[16,12]{1,0:T(8,128)S(1)}, s32[16,12]{1,0:T(8,128)}, u32[]{:S(2)}) %copy-start.1) | copy-done | bytes 792
  3.3 0.0 copy-start.2
  3.3 0.7 %copy-done.2 = f32[12]{0:T(128)S(1)} copy-done((f32[12]{0:T(128)S(1)}, f32[12]{0:T(128)}, u32[]{:S(2)}) %copy-start.2) | copy-done | bytes 72
  4.0 0.0 copy-start.3
  4.0 0.7 %copy-done.3 = s32[8]{0:T(128)S(1)} copy-done((s32[8]{0:T(128)S(1)}, s32[8]{0:T(128)}, u32[]{:S(2)}) %copy-start.3) | copy-done | bytes 56
  4.6 0.0 copy-start.4
  4.6 0.7 %copy-done.4 = s32[8]{0:T(128)S(1)} copy-done((s32[8]{0:T(128)S(1)}, s32[8]{0:T(128)}, u32[]{:S(2)}) %copy-start.4) | copy-done | bytes 56
  5.3 0.0 copy-start.5
  5.3 0.7 %copy-done.5 = s32[14]{0:T(128)S(1)} copy-done((s32[14]{0:T(128)S(1)}, s32[14]{0:T(128)}, u32[]{:S(2)}) %copy-start.5) | copy-done | bytes 80
  5.9 0.0 copy-start.6
  5.9 0.7 %copy-done.6 = f32[8]{0:T(128)S(1)} copy-done((f32[8]{0:T(128)S(1)}, f32[8]{0:T(128)}, u32[]{:S(2)}) %copy-start.6) | copy-done | bytes 56
  6.6 0.0 copy-start.7
  6.6 0.7 %copy-done.7 = s32[4]{0:T(128)S(1)} copy-done((s32[4]{0:T(128)S(1)}, s32[4]{0:T(128)}, u32[]{:S(2)}) %copy-start.7) | copy-done | bytes 40
  7.3 0.0 copy-start.8
  7.3 0.7 %copy-done.8 = f32[4]{0:T(128)S(1)} copy-done((f32[4]{0:T(128)S(1)}, f32[4]{0:T(128)}, u32[]{:S(2)}) %copy-start.8) | copy-done | bytes 40
  7.9 40.0 %shard_map.122 = (f32[1,1,128,2048]{3,2,1,0:T(8,128)S(1)}, f32[1,1,128,2048]{3,2,1,0:T(8,128)S(1)}) custom-call(f32[1,1,128,2048]{3,2,1,0:T(8,128)S(1)} %copy-done, bf16[16,12,128,128]{3,2,1,0:T(8,128)(2,1)} %block_values.1, s32[16,12]{1,0:T(8,128)S(1)} %copy-done.1, s32[12,2]{1,0:T(8,128)S(1)} %copy.13.bond_sites, f32[12]{0:T(128)S(1)} %copy-done.2, ...), custom_call_target="tpu_custom_call" | custom-call | tf_op jit(solution)/shard_map/pallas_call | solution.py:254
  47.9 1.0 %copy.16 = f32[1,1,128,2048]{3,2,1,0:T(8,128)} copy(f32[1,1,128,2048]{3,2,1,0:T(8,128)S(1)} %get-tuple-element.4) | data formatting | bytes 2097152
  48.9 1.0 %copy.17 = f32[1,1,128,2048]{3,2,1,0:T(8,128)} copy(f32[1,1,128,2048]{3,2,1,0:T(8,128)S(1)} %get-tuple-element.5) | data formatting | bytes 2097152
Async XLA Ops:
  1.4 1.2 %copy-start = (f32[1,1,128,2048]{3,2,1,0:T(8,128)S(1)}, f32[1,1,128,2048]{3,2,1,0:T(8,128)}, u32[]{:S(2)}) copy-start(f32[1,1,128,2048]{3,2,1,0:T(8,128)} %initial.1) | copy-start | bytes 3145732
  2.6 0.7 %copy-start.1 = (s32[16,12]{1,0:T(8,128)S(1)}, s32[16,12]{1,0:T(8,128)}, u32[]{:S(2)}) copy-start(s32[16,12]{1,0:T(8,128)} %block_index.1) | copy-start | bytes 2308
  3.3 0.7 %copy-start.2 = (f32[12]{0:T(128)S(1)}, f32[12]{0:T(128)}, u32[]{:S(2)}) copy-start(f32[12]{0:T(128)} %bond_coupling.1) | copy-start | bytes 148
  4.0 0.7 %copy-start.3 = (s32[8]{0:T(128)S(1)}, s32[8]{0:T(128)}, u32[]{:S(2)}) copy-start(s32[8]{0:T(128)} %pin_sites.1) | copy-start | bytes 100
  4.6 0.7 %copy-start.4 = (s32[8]{0:T(128)S(1)}, s32[8]{0:T(128)}, u32[]{:S(2)}) copy-start(s32[8]{0:T(128)} %pin_partner.1) | copy-start | bytes 100
  5.3 0.7 %copy-start.5 = (s32[14]{0:T(128)S(1)}, s32[14]{0:T(128)}, u32[]{:S(2)}) copy-start(s32[14]{0:T(128)} %pinned_spins.1) | copy-start | bytes 172
  5.9 0.7 %copy-start.6 = (f32[8]{0:T(128)S(1)}, f32[8]{0:T(128)}, u32[]{:S(2)}) copy-start(f32[8]{0:T(128)} %pin_coupling.1) | copy-start | bytes 100
  6.6 0.7 %copy-start.7 = (s32[4]{0:T(128)S(1)}, s32[4]{0:T(128)}, u32[]{:S(2)}) copy-start(s32[4]{0:T(128)} %cross_sites.1) | copy-start | bytes 52
  7.3 0.7 %copy-start.8 = (f32[4]{0:T(128)S(1)}, f32[4]{0:T(128)}, u32[]{:S(2)}) copy-start(f32[4]{0:T(128)} %cross_coupling.1) | copy-start | bytes 52
where the time goes:
time: 50.1 us; the launch traced here: 49.8 us
  Pallas kernels  40 us (80%)
  local copies, waits for them, and re-layouts  9.21 us (18%)
  between operations  0.65 us (1%)
    pallas_call x1, Pallas kernels, shards(): pl.pallas_call(functools.partial(kernel, sizes), out_shape=(whole, whole)...  40 us
    unnamed x21, local copies, waits for them, and re-layouts  9.21 us

commit v1 on v0

v1 whole, which is shorter than its diff:
```python
import functools

import jax
import jax.numpy as jnp
from jax import lax
from jax.experimental import pallas as pl
from jax.experimental.pallas import tpu as pltpu
from jax.sharding import PartitionSpec as P

MESH = pl.DeviceIdType.MESH
STEPS = 4
CROSS = 4
CHUNK = 256


def bit_at(values, position):
    return jnp.bitwise_and(jnp.right_shift(values, position), 1)


def squeezed(columns, site):
    kept = jnp.bitwise_and(columns, jnp.left_shift(1, site) - 1)
    return kept | jnp.left_shift(jnp.right_shift(columns, site + 1), site)


def spread(packed, site, bit):
    kept = jnp.bitwise_and(packed, jnp.left_shift(1, site) - 1)
    high = jnp.left_shift(jnp.right_shift(packed, site), site + 1)
    return high | kept | jnp.left_shift(bit, site)


def lanes(count):
    return lax.broadcasted_iota(jnp.int32, (1, count), 1)


def rows_of(count, width):
    return lax.broadcasted_iota(jnp.int32, (count, width), 0)


def split(values):
    scaled = values * 65537.0
    high = scaled - (scaled - values)
    return high, values - high


def kernel(
    sizes,
    initial,
    block_values,
    *refs,
):
    smalls, (previous_out, current_out), refs = refs[:9], refs[9:11], refs[11:]
    (
        block_index,
        bond_sites,
        bond_coupling,
        pin_sites,
        pin_partner,
        pinned_spins,
        pin_coupling,
        cross_sites,
        cross_coupling,
    ) = refs[:9]
    (
        values,
        dense,
        states,
        high,
        low,
        ahead,
        sent,
        received,
        mixer,
        crosser,
        picker,
        small_sem,
        load_sem,
        value_sem,
        send_sem,
        recv_sem,
    ) = refs[9:]
    wide_log, narrow_log, columns, chunks, kept, bonds, pins = sizes
    rows = 2 * chunks
    half = columns // 2
    wide, narrow = lax.axis_index("wide"), lax.axis_index("narrow")
    own_bits = (
        bit_at(wide, wide_log - 1),
        bit_at(wide, 0),
        bit_at(narrow, narrow_log - 1),
        bit_at(narrow, 0),
    )

    def flipped(index, bit, position):
        return index + (1 - 2 * bit) * (1 << position)

    partners = (
        (flipped(wide, own_bits[0], wide_log - 1), narrow),
        (flipped(wide, own_bits[1], 0), narrow),
        (wide, flipped(narrow, own_bits[2], narrow_log - 1)),
        (wide, flipped(narrow, own_bits[3], 0)),
    )
    barrier = pltpu.get_barrier_semaphore()
    for partner in partners:
        pl.semaphore_signal(barrier, inc=1, device_id=partner, device_id_type=MESH)

    def load_small(i):
        return pltpu.make_async_copy(smalls[i], refs[i], small_sem.at[i])

    def load(j):
        return pltpu.make_async_copy(
            initial.at[0, 0, :, pl.ds(pl.multiple_of(j * CHUNK, CHUNK), CHUNK)],
            states.at[1, j],
            load_sem.at[j],
        )

    def load_values(j):
        pair = pl.ds(2 * j, 2)
        return pltpu.make_async_copy(
            block_values.at[pair], values.at[pair, pl.ds(0, kept)], value_sem.at[j]
        )

    def exchange(step, j, k):
        return pltpu.make_async_remote_copy(
            src_ref=sent.at[step, j, k],
            dst_ref=received.at[step, j, k],
            send_sem=send_sem.at[step, j, k],
            recv_sem=recv_sem.at[step, j, k],
            device_id=partners[k],
            device_id_type=MESH,
        )

    def store(out, j, state):
        out[0, 0, :, pl.ds(pl.multiple_of(j * CHUNK, CHUNK), CHUNK)] = state

    def keep(step, j, state):
        rounded = state.astype(jnp.bfloat16)
        rest = (state - rounded.astype(jnp.float32)).astype(jnp.bfloat16)
        for pair in range(CROSS // 2):
            wanted = picker[pair * columns : pair * columns + columns, :]
            packed = jnp.dot(wanted, rounded, preferred_element_type=jnp.float32)
            packed = packed.astype(jnp.bfloat16)
            for k in range(2):
                for h in range(2):
                    sent[step, j, 2 * pair + k, h] = packed[
                        k * half : k * half + half, h * 128 : h * 128 + 128
                    ]
        for h in range(2):
            high[step, 2 * j + h] = rounded[:, h * 128 : h * 128 + 128]
            low[step, 2 * j + h] = rest[:, h * 128 : h * 128 + 128]

    def send(step, j):
        for k in range(CROSS):
            exchange(step, j, k).start()

    for i in range(9):
        load_small(i).start()
    for j in range(chunks):
        load(j).start()
    for j in range(chunks):
        load_values(j).start()
    for i in range(9):
        load_small(i).wait()

    sites = [cross_sites[k] for k in range(CROSS)]
    column = lanes(columns)
    for k in range(CROSS):
        places = jnp.where(
            bit_at(column, sites[k]) == own_bits[k], -1, squeezed(column, sites[k])
        )
        chosen = rows_of(half, columns) == places
        picker[k * half : k * half + half, :] = jnp.where(chosen, 1.0, 0.0).astype(jnp.bfloat16)

    @pl.loop(0, chunks)
    def _(j):
        load(j).wait()
        keep(0, j, states[1, j])

    pl.semaphore_wait(barrier, CROSS)

    @pl.loop(0, chunks)
    def _(j):
        send(0, j)

    crossing = [[], []]
    for pair in range(CROSS // 2):
        upper = lanes(columns) >= half
        one, two = 2 * pair, 2 * pair + 1

        def either(first, second):
            return jnp.where(upper, second, first)

        arriving = spread(
            jnp.bitwise_and(lanes(columns), half - 1),
            either(sites[one], sites[two]),
            either(1 - own_bits[one], 1 - own_bits[two]),
        )
        met = rows_of(columns, columns) == arriving
        strengths = zip(split(cross_coupling[one] * 0.5), split(cross_coupling[two] * 0.5))
        for part, (first, second) in zip(crossing, strengths):
            part.append(jnp.where(met, either(first, second), 0.0).astype(jnp.bfloat16))
    for i in range(2):
        crosser[i] = jnp.concatenate(crossing[i], axis=1)

    row = rows_of(columns, columns)
    hopping = jnp.zeros((columns, columns), jnp.float32)
    diagonal = jnp.zeros((1, columns), jnp.float32)
    for b in range(bonds):
        one, two = bond_sites[0, b], bond_sites[1, b]
        differ = jnp.bitwise_xor(bit_at(column, one), bit_at(column, two)).astype(jnp.float32)
        source = jnp.bitwise_xor(column, jnp.left_shift(1, one) ^ jnp.left_shift(1, two))
        hopping += jnp.where(row == source, bond_coupling[b] * 0.5 * differ, 0.0)
        diagonal += bond_coupling[b] * 0.25 * (1.0 - 2.0 * differ)
    for p in range(pins):
        aligned = jnp.bitwise_xor(bit_at(column, pin_sites[p]), pinned_spins[pin_partner[p]])
        diagonal += pin_coupling[p] * 0.25 * (1.0 - 2.0 * aligned.astype(jnp.float32))
    for k in range(CROSS):
        parity = jnp.bitwise_xor(bit_at(column, sites[k]), own_bits[k])
        diagonal += cross_coupling[k] * 0.25 * (1.0 - 2.0 * parity.astype(jnp.float32))
    matrix = [
        part.astype(jnp.bfloat16) for part in split(hopping + jnp.where(row == column, diagonal, 0.0))
    ]
    mixer[...] = jnp.concatenate([matrix[0], matrix[0], matrix[1]], axis=1)
    states[0] = jnp.zeros(states.shape[1:], jnp.float32)
    values[:, kept] = jnp.zeros((rows, 128, 128), jnp.bfloat16)

    for j in range(chunks):
        load_values(j).wait()

    @pl.loop(0, chunks)
    def _(j):
        for part in range(2):
            r = 2 * j + part
            empty = sum(kept << 4 * i for i in range(8))
            places = [jnp.int32(empty - (1 << 32) if empty >> 31 else empty)] * 2
            for q in range(kept):
                wanted = block_index[r, q]
                shift = 4 * jnp.bitwise_and(wanted, 7)
                moved = jnp.left_shift(jnp.int32(q - kept), shift)
                upper = wanted >= 8
                places = [
                    places[0] + jnp.where(upper, 0, moved),
                    places[1] + jnp.where(upper, moved, 0),
                ]
            for m in range(rows):
                q = jnp.bitwise_and(jnp.right_shift(places[m // 8], 4 * (m % 8)), 15)
                dense[j, part, m] = values[r, jnp.minimum(q, kept)]

    def own_product(step, j):
        left = jnp.concatenate([high[step, m] for m in range(rows)] + [mixer[...]], axis=1)
        right = []
        for h in range(2):
            own_high, own_low = high[step, 2 * j + h], low[step, 2 * j + h]
            blocks = dense[j, h].reshape(rows * 128, 128)
            right.append(jnp.concatenate([blocks, own_high, own_low, own_high], axis=0))
        return jnp.dot(left, jnp.concatenate(right, axis=1), preferred_element_type=jnp.float32)

    def next_state(step, j, scale):
        arrived = jnp.concatenate(
            [received[step, j, :, h].reshape(CROSS * half, 128) for h in range(2)], axis=1
        )
        total = ahead[...]
        for i in range(2):
            total += jnp.dot(crosser[i], arrived, preferred_element_type=jnp.float32)
        return scale * total - states[step, j]

    def arrive(step, j):
        for k in range(CROSS):
            exchange(step, j, k).wait_recv()

    @pl.loop(0, STEPS - 1)
    def _(step):
        scale = jnp.where(step == 0, 1.0, 2.0)

        def advance(j):
            arrive(step, j)
            state = next_state(step, j, scale)
            states[step + 2, j] = state
            keep(step + 1, j, state)

        ahead[...] = own_product(step, 0)

        @pl.loop(0, chunks - 1)
        def _(j):
            advance(j)
            ahead[...] = own_product(step, j + 1)
            send(step + 1, j)

        advance(chunks - 1)
        send(step + 1, chunks - 1)

    last = STEPS - 1
    ahead[...] = own_product(last, 0)

    @pl.loop(0, chunks - 1)
    def _(j):
        store(previous_out, j, states[STEPS, j])
        arrive(last, j)
        store(current_out, j, next_state(last, j, 2.0))
        ahead[...] = own_product(last, j + 1)

    store(previous_out, chunks - 1, states[STEPS, chunks - 1])
    arrive(last, chunks - 1)
    store(current_out, chunks - 1, next_state(last, chunks - 1, 2.0))

    @pl.loop(0, STEPS)
    def _(step):
        @pl.loop(0, chunks)
        def _(j):
            for k in range(CROSS):
                exchange(step, j, k).wait_send()


def leave(previous, current, previous_out, current_out, sem):
    copies = [
        pltpu.make_async_copy(previous, previous_out, sem.at[0]),
        pltpu.make_async_copy(current, current_out, sem.at[1]),
    ]
    for copy in copies:
        copy.start()
    for copy in copies:
        copy.wait()


def solution(mesh):
    wide_log = mesh.shape["wide"].bit_length() - 1
    narrow_log = mesh.shape["narrow"].bit_length() - 1

    def shards(initial, block_values, block_index, bond_sites, *rest):
        columns, width = initial.shape[2:]
        rows, kept = block_index.shape
        chunks = width // CHUNK
        sizes = (
            wide_log,
            narrow_log,
            columns,
            chunks,
            kept,
            bond_sites.shape[0],
            rest[1].shape[0],
        )
        whole = jax.ShapeDtypeStruct(initial.shape, jnp.float32)
        half_rows = CROSS * columns // 2
        smalls = (block_index, bond_sites.T, *rest)
        parts = pl.pallas_call(
            functools.partial(kernel, sizes),
            out_shape=(whole, whole),
            in_specs=[pl.BlockSpec(memory_space=pltpu.HBM)] * (2 + len(smalls)),
            out_specs=(pl.BlockSpec(memory_space=pltpu.VMEM),) * 2,
            scratch_shapes=[pltpu.SMEM(small.shape, small.dtype) for small in smalls]
            + [
                pltpu.VMEM((rows, kept + 1, 128, 128), jnp.bfloat16),
                pltpu.VMEM((chunks, 2, rows, 128, 128), jnp.bfloat16),
                pltpu.VMEM((STEPS + 1, chunks, columns, CHUNK), jnp.float32),
                pltpu.VMEM((STEPS, rows, columns, 128), jnp.bfloat16),
                pltpu.VMEM((STEPS, rows, columns, 128), jnp.bfloat16),
                pltpu.VMEM((columns, CHUNK), jnp.float32),
                pltpu.VMEM((STEPS, chunks, CROSS, 2, columns // 2, 128), jnp.bfloat16),
                pltpu.VMEM((STEPS, chunks, CROSS, 2, columns // 2, 128), jnp.bfloat16),
                pltpu.VMEM((columns, 3 * columns), jnp.bfloat16),
                pltpu.VMEM((2, columns, half_rows), jnp.bfloat16),
                pltpu.VMEM((half_rows, columns), jnp.bfloat16),
                pltpu.SemaphoreType.DMA((len(smalls),)),
                pltpu.SemaphoreType.DMA((chunks,)),
                pltpu.SemaphoreType.DMA((chunks,)),
                pltpu.SemaphoreType.DMA((STEPS, chunks, CROSS)),
                pltpu.SemaphoreType.DMA((STEPS, chunks, CROSS)),
            ],
            compiler_params=pltpu.CompilerParams(
                collective_id=0, has_side_effects=True, vmem_limit_bytes=48 * 1024 * 1024
            ),
        )(*[pltpu.with_memory_space_constraint(a, pltpu.HBM) for a in (initial, block_values, *smalls)])
        return pl.pallas_call(
            leave,
            out_shape=(whole, whole),
            in_specs=[pl.BlockSpec(memory_space=pl.ANY)] * 2,
            out_specs=(pl.BlockSpec(memory_space=pltpu.HBM),) * 2,
            scratch_shapes=[pltpu.SemaphoreType.DMA((2,))],
            compiler_params=pltpu.CompilerParams(vmem_limit_bytes=1024 * 1024),
        )(*parts)

    slab = P("wide", "narrow", None, None)
    return jax.shard_map(
        shards,
        mesh=mesh,
        in_specs=(slab,) + (P(),) * 10,
        out_specs=(slab, slab),
        check_vma=False,
    )
```

time: 50.1 us -> 35.3 us (0.70)
  local copies, waits for them, and re-layouts: 9.21 us -> 0 us
  Pallas kernels: 40 us -> 34.5 us
    unnamed x21 -> x0, local copies, waits for them, and re-layouts: 9.21 us -> none
    pallas_call x1, Pallas kernels: 40 us -> 33.2 us  [shards(): pl.pallas_call(functools.partial(kernel, sizes), out_shape=(whole, whole)...]
    pallas_call x0 -> x1, Pallas kernels: none -> 1.33 us  [shards(): pl.pallas_call(leave, out_shape=(whole, whole), in_specs=[pl.BlockSpec(me...]
where the time goes in v1:
time: 35.3 us; the launch traced here: 35.2 us
  Pallas kernels  34.5 us (98%)
  between operations  0.64 us (2%)
    pallas_call x1, Pallas kernels, shards(): pl.pallas_call(functools.partial(kernel, sizes), out_shape=(whole, whole)...  33.2 us
    pallas_call x1, Pallas kernels, shards(): pl.pallas_call(leave, out_shape=(whole, whole), in_specs=[pl.BlockSpec(me...  1.33 us

profile of v1, /device:TPU:64, one launch (start us, length us, event | category | flops | bytes accessed | tf_op | source)
XLA Modules:
  0.0 35.2 jit_solution(8977606217524871537)
XLA Ops:
  0.6 33.2 %shard_map.122 = (f32[1,1,128,2048]{3,2,1,0:T(8,128)S(1)}, f32[1,1,128,2048]{3,2,1,0:T(8,128)S(1)}) custom-call(f32[1,1,128,2048]{3,2,1,0:T(8,128)} %initial.1, bf16[16,12,128,128]{3,2,1,0:T(8,128)(2,1)} %block_values.1, s32[16,12]{1,0:T(8,128)} %refs_0_.1, s32[2,12]{1,0:T(2,128)} %bitcast.1, f32[12]{0:T(128)} %refs_2_.1, s32[8]{0:T(128)} %refs_3_.1, ...), custom_call_target="tpu_custom_call" | custom-call | tf_op jit(solution)/shard_map/pallas_call | solution.py:343
  33.8 1.3 %shard_map.123 = (f32[1,1,128,2048]{3,2,1,0:T(8,128)}, f32[1,1,128,2048]{3,2,1,0:T(8,128)}) custom-call(f32[1,1,128,2048]{3,2,1,0:T(8,128)S(1)} %get-tuple-element.4.previous, f32[1,1,128,2048]{3,2,1,0:T(8,128)S(1)} %get-tuple-element.5.current), custom_call_target="tpu_custom_call" | custom-call | tf_op jit(solution)/shard_map/pallas_call | solution.py:371

commit v2 on v1

--- a/solution.py
+++ b/solution.py
@@ -10,7 +10,8 @@
 MESH = pl.DeviceIdType.MESH
 STEPS = 4
 CROSS = 4
-CHUNK = 256
+CHUNK = 512
+PARTS = CHUNK // 128
 
 
 def bit_at(values, position):
@@ -79,7 +80,7 @@
         recv_sem,
     ) = refs[9:]
     wide_log, narrow_log, columns, chunks, kept, bonds, pins = sizes
-    rows = 2 * chunks
+    rows = PARTS * chunks
     half = columns // 2
     wide, narrow = lax.axis_index("wide"), lax.axis_index("narrow")
     own_bits = (
@@ -113,9 +114,9 @@
         )
 
     def load_values(j):
-        pair = pl.ds(2 * j, 2)
+        some = pl.ds(PARTS * j, PARTS)
         return pltpu.make_async_copy(
-            block_values.at[pair], values.at[pair, pl.ds(0, kept)], value_sem.at[j]
+            block_values.at[some], values.at[some, pl.ds(0, kept)], value_sem.at[j]
         )
 
     def exchange(step, j, k):
@@ -134,18 +135,14 @@
     def keep(step, j, state):
         rounded = state.astype(jnp.bfloat16)
         rest = (state - rounded.astype(jnp.float32)).astype(jnp.bfloat16)
-        for pair in range(CROSS // 2):
-            wanted = picker[pair * columns : pair * columns + columns, :]
-            packed = jnp.dot(wanted, rounded, preferred_element_type=jnp.float32)
-            packed = packed.astype(jnp.bfloat16)
-            for k in range(2):
-                for h in range(2):
-                    sent[step, j, 2 * pair + k, h] = packed[
-                        k * half : k * half + half, h * 128 : h * 128 + 128
-                    ]
-        for h in range(2):
-            high[step, 2 * j + h] = rounded[:, h * 128 : h * 128 + 128]
-            low[step, 2 * j + h] = rest[:, h * 128 : h * 128 + 128]
+        packed = jnp.dot(picker[...], rounded, preferred_element_type=jnp.float32)
+        packed = packed.astype(jnp.bfloat16)
+        for h in range(PARTS):
+            lanes_of = slice(h * 128, h * 128 + 128)
+            high[step, PARTS * j + h] = rounded[:, lanes_of]
+            low[step, PARTS * j + h] = rest[:, lanes_of]
+            for k in range(CROSS):
+                sent[step, j, k, h] = packed[k * half : k * half + half, lanes_of]
 
     def send(step, j):
         for k in range(CROSS):
@@ -169,15 +166,12 @@
         chosen = rows_of(half, columns) == places
         picker[k * half : k * half + half, :] = jnp.where(chosen, 1.0, 0.0).astype(jnp.bfloat16)
 
+    pl.semaphore_wait(barrier, CROSS)
+
     @pl.loop(0, chunks)
     def _(j):
         load(j).wait()
         keep(0, j, states[1, j])
-
-    pl.semaphore_wait(barrier, CROSS)
-
-    @pl.loop(0, chunks)
-    def _(j):
         send(0, j)
 
     crossing = [[], []]
@@ -198,7 +192,7 @@
         for part, (first, second) in zip(crossing, strengths):
             part.append(jnp.where(met, either(first, second), 0.0).astype(jnp.bfloat16))
     for i in range(2):
-        crosser[i] = jnp.concatenate(crossing[i], axis=1)
+        crosser[i * columns : i * columns + columns, :] = jnp.concatenate(crossing[i], axis=1)
 
     row = rows_of(columns, columns)
     hopping = jnp.zeros((columns, columns), jnp.float32)
@@ -227,8 +221,8 @@
 
     @pl.loop(0, chunks)
     def _(j):
-        for part in range(2):
-            r = 2 * j + part
+        for part in range(PARTS):
+            r = PARTS * j + part
             empty = sum(kept << 4 * i for i in range(8))
             places = [jnp.int32(empty - (1 << 32) if empty >> 31 else empty)] * 2
             for q in range(kept):
@@ -247,24 +241,25 @@
     def own_product(step, j):
         left = jnp.concatenate([high[step, m] for m in range(rows)] + [mixer[...]], axis=1)
         right = []
-        for h in range(2):
-            own_high, own_low = high[step, 2 * j + h], low[step, 2 * j + h]
+        for h in range(PARTS):
+            own_high, own_low = high[step, PARTS * j + h], low[step, PARTS * j + h]
             blocks = dense[j, h].reshape(rows * 128, 128)
             right.append(jnp.concatenate([blocks, own_high, own_low, own_high], axis=0))
         return jnp.dot(left, jnp.concatenate(right, axis=1), preferred_element_type=jnp.float32)
 
-    def next_state(step, j, scale):
+    def crossing_product(step, j):
         arrived = jnp.concatenate(
-            [received[step, j, :, h].reshape(CROSS * half, 128) for h in range(2)], axis=1
-        )
-        total = ahead[...]
-        for i in range(2):
-            total += jnp.dot(crosser[i], arrived, preferred_element_type=jnp.float32)
-        return scale * total - states[step, j]
+            [received[step, j, :, h].reshape(CROSS * half, 128) for h in range(PARTS)], axis=1
+        )
+        both = jnp.dot(crosser[...], arrived, preferred_element_type=jnp.float32)
+        return both[:columns] + both[columns:]
 
     def arrive(step, j):
         for k in range(CROSS):
             exchange(step, j, k).wait_recv()
+
+    def next_state(step, j, scale):
+        return scale * (ahead[...] + crossing_product(step, j)) - states[step, j]
 
     @pl.loop(0, STEPS - 1)
     def _(step):
@@ -348,15 +343,15 @@
             scratch_shapes=[pltpu.SMEM(small.shape, small.dtype) for small in smalls]
             + [
                 pltpu.VMEM((rows, kept + 1, 128, 128), jnp.bfloat16),
-                pltpu.VMEM((chunks, 2, rows, 128, 128), jnp.bfloat16),
+                pltpu.VMEM((chunks, PARTS, rows, 128, 128), jnp.bfloat16),
                 pltpu.VMEM((STEPS + 1, chunks, columns, CHUNK), jnp.float32),
                 pltpu.VMEM((STEPS, rows, columns, 128), jnp.bfloat16),
                 pltpu.VMEM((STEPS, rows, columns, 128), jnp.bfloat16),
                 pltpu.VMEM((columns, CHUNK), jnp.float32),
-                pltpu.VMEM((STEPS, chunks, CROSS, 2, columns // 2, 128), jnp.bfloat16),
-                pltpu.VMEM((STEPS, chunks, CROSS, 2, columns // 2, 128), jnp.bfloat16),
+                pltpu.VMEM((STEPS, chunks, CROSS, PARTS, columns // 2, 128), jnp.bfloat16),
+                pltpu.VMEM((STEPS, chunks, CROSS, PARTS, columns // 2, 128), jnp.bfloat16),
                 pltpu.VMEM((columns, 3 * columns), jnp.bfloat16),
-                pltpu.VMEM((2, columns, half_rows), jnp.bfloat16),
+                pltpu.VMEM((2 * columns, half_rows), jnp.bfloat16),
                 pltpu.VMEM((half_rows, columns), jnp.bfloat16),
                 pltpu.SemaphoreType.DMA((len(smalls),)),
                 pltpu.SemaphoreType.DMA((chunks,)),

time: 35.3 us -> 33.4 us (0.946)
  Pallas kernels: 34.5 us -> 32.7 us
    pallas_call x1, Pallas kernels: 33.2 us -> 31.3 us  [shards(): pl.pallas_call(functools.partial(kernel, sizes), out_shape=(whole, whole)...]
where the time goes in v2:
time: 33.4 us; the launch traced here: 33.3 us
  Pallas kernels  32.7 us (98%)
  between operations  0.64 us (2%)
    pallas_call x1, Pallas kernels, shards(): pl.pallas_call(functools.partial(kernel, sizes), out_shape=(whole, whole)...  31.3 us
    pallas_call x1, Pallas kernels, shards(): pl.pallas_call(leave, out_shape=(whole, whole), in_specs=[pl.BlockSpec(me...  1.33 us

profile of v2, /device:TPU:64, one launch (start us, length us, event | category | flops | bytes accessed | tf_op | source)
XLA Modules:
  0.0 33.3 jit_solution(9741870489746942023)
XLA Ops:
  0.6 31.3 %shard_map.122 = (f32[1,1,128,2048]{3,2,1,0:T(8,128)S(1)}, f32[1,1,128,2048]{3,2,1,0:T(8,128)S(1)}) custom-call(f32[1,1,128,2048]{3,2,1,0:T(8,128)} %initial.1, bf16[16,12,128,128]{3,2,1,0:T(8,128)(2,1)} %block_values.1, s32[16,12]{1,0:T(8,128)} %refs_0_.1, s32[2,12]{1,0:T(2,128)} %bitcast.1, f32[12]{0:T(128)} %refs_2_.1, s32[8]{0:T(128)} %refs_3_.1, ...), custom_call_target="tpu_custom_call" | custom-call | tf_op jit(solution)/shard_map/pallas_call | solution.py:338
  32.0 1.3 %shard_map.123 = (f32[1,1,128,2048]{3,2,1,0:T(8,128)}, f32[1,1,128,2048]{3,2,1,0:T(8,128)}) custom-call(f32[1,1,128,2048]{3,2,1,0:T(8,128)S(1)} %get-tuple-element.4.previous, f32[1,1,128,2048]{3,2,1,0:T(8,128)S(1)} %get-tuple-element.5.current), custom_call_target="tpu_custom_call" | custom-call | tf_op jit(solution)/shard_map/pallas_call | solution.py:366

commit v3 on v2

--- a/solution.py
+++ b/solution.py
@@ -12,6 +12,7 @@
 CROSS = 4
 CHUNK = 512
 PARTS = CHUNK // 128
+EARLY = 8
 
 
 def bit_at(values, position):
@@ -116,18 +117,26 @@
     def load_values(j):
         some = pl.ds(PARTS * j, PARTS)
         return pltpu.make_async_copy(
-            block_values.at[some], values.at[some, pl.ds(0, kept)], value_sem.at[j]
+            block_values.at[some], values.at[some, pl.ds(0, kept)], value_sem.at[0]
         )
 
     def exchange(step, j, k):
         return pltpu.make_async_remote_copy(
             src_ref=sent.at[step, j, k],
             dst_ref=received.at[step, j, k],
-            send_sem=send_sem.at[step, j, k],
-            recv_sem=recv_sem.at[step, j, k],
+            send_sem=send_sem.at[step],
+            recv_sem=recv_sem.at[lax.rem(step, 2), j],
             device_id=partners[k],
             device_id_type=MESH,
         )
+
+    def arrival(step, j):
+        every = received.at[step, j]
+        return pltpu.make_async_copy(every, every, recv_sem.at[lax.rem(step, 2), j])
+
+    def departure(step):
+        every = sent.at[step]
+        return pltpu.make_async_copy(every, every, send_sem.at[step])
 
     def store(out, j, state):
         out[0, 0, :, pl.ds(pl.multiple_of(j * CHUNK, CHUNK), CHUNK)] = state
@@ -216,8 +225,8 @@
     states[0] = jnp.zeros(states.shape[1:], jnp.float32)
     values[:, kept] = jnp.zeros((rows, 128, 128), jnp.bfloat16)
 
-    for j in range(chunks):
-        load_values(j).wait()
+    every = values.at[:, pl.ds(0, kept)]
+    pltpu.make_async_copy(every, every, value_sem.at[0]).wait()
 
     @pl.loop(0, chunks)
     def _(j):
@@ -238,14 +247,22 @@
                 q = jnp.bitwise_and(jnp.right_shift(places[m // 8], 4 * (m % 8)), 15)
                 dense[j, part, m] = values[r, jnp.minimum(q, kept)]
 
-    def own_product(step, j):
-        left = jnp.concatenate([high[step, m] for m in range(rows)] + [mixer[...]], axis=1)
+    def own_product(step, j, first, count, column):
+        left = [high[step, first + m] for m in range(count)]
+        if column:
+            left.append(mixer[...])
         right = []
         for h in range(PARTS):
-            own_high, own_low = high[step, PARTS * j + h], low[step, PARTS * j + h]
-            blocks = dense[j, h].reshape(rows * 128, 128)
-            right.append(jnp.concatenate([blocks, own_high, own_low, own_high], axis=0))
-        return jnp.dot(left, jnp.concatenate(right, axis=1), preferred_element_type=jnp.float32)
+            blocks = [dense[j, h, first : first + count].reshape(count * 128, 128)]
+            if column:
+                own_high, own_low = high[step, PARTS * j + h], low[step, PARTS * j + h]
+                blocks += [own_high, own_low, own_high]
+            right.append(jnp.concatenate(blocks, axis=0))
+        return jnp.dot(
+            jnp.concatenate(left, axis=1),
+            jnp.concatenate(right, axis=1),
+            preferred_element_type=jnp.float32,
+        )
 
     def crossing_product(step, j):
         arrived = jnp.concatenate(
@@ -255,11 +272,12 @@
         return both[:columns] + both[columns:]
 
     def arrive(step, j):
-        for k in range(CROSS):
-            exchange(step, j, k).wait_recv()
+        arrival(step, j).wait()
 
     def next_state(step, j, scale):
         return scale * (ahead[...] + crossing_product(step, j)) - states[step, j]
+
+    ahead[...] = own_product(0, 0, 0, rows, True)
 
     @pl.loop(0, STEPS - 1)
     def _(step):
@@ -271,37 +289,33 @@
             states[step + 2, j] = state
             keep(step + 1, j, state)
 
-        ahead[...] = own_product(step, 0)
-
         @pl.loop(0, chunks - 1)
         def _(j):
             advance(j)
-            ahead[...] = own_product(step, j + 1)
+            ahead[...] = own_product(step, j + 1, 0, EARLY, True)
             send(step + 1, j)
+            ahead[...] += own_product(step, j + 1, EARLY, rows - EARLY, False)
 
         advance(chunks - 1)
+        ahead[...] = own_product(step + 1, 0, 0, rows - PARTS, True)
         send(step + 1, chunks - 1)
+        ahead[...] += own_product(step + 1, 0, rows - PARTS, PARTS, False)
 
     last = STEPS - 1
-    ahead[...] = own_product(last, 0)
 
     @pl.loop(0, chunks - 1)
     def _(j):
         store(previous_out, j, states[STEPS, j])
         arrive(last, j)
         store(current_out, j, next_state(last, j, 2.0))
-        ahead[...] = own_product(last, j + 1)
+        ahead[...] = own_product(last, j + 1, 0, rows, True)
 
     store(previous_out, chunks - 1, states[STEPS, chunks - 1])
     arrive(last, chunks - 1)
     store(current_out, chunks - 1, next_state(last, chunks - 1, 2.0))
 
-    @pl.loop(0, STEPS)
-    def _(step):
-        @pl.loop(0, chunks)
-        def _(j):
-            for k in range(CROSS):
-                exchange(step, j, k).wait_send()
+    for step in range(STEPS):
+        departure(step).wait()
 
 
 def leave(previous, current, previous_out, current_out, sem):
@@ -355,9 +369,9 @@
                 pltpu.VMEM((half_rows, columns), jnp.bfloat16),
                 pltpu.SemaphoreType.DMA((len(smalls),)),
                 pltpu.SemaphoreType.DMA((chunks,)),
-                pltpu.SemaphoreType.DMA((chunks,)),
-                pltpu.SemaphoreType.DMA((STEPS, chunks, CROSS)),
-                pltpu.SemaphoreType.DMA((STEPS, chunks, CROSS)),
+                pltpu.SemaphoreType.DMA((1,)),
+                pltpu.SemaphoreType.DMA((STEPS,)),
+                pltpu.SemaphoreType.DMA((2, chunks)),
             ],
             compiler_params=pltpu.CompilerParams(
                 collective_id=0, has_side_effects=True, vmem_limit_bytes=48 * 1024 * 1024

time: 33.4 us -> 32.2 us (0.964)
  Pallas kernels: 32.7 us -> 31.5 us
    pallas_call x1, Pallas kernels: 31.3 us -> 30.1 us  [shards(): pl.pallas_call(functools.partial(kernel, sizes), out_shape=(whole, whole)...]
where the time goes in v3:
time: 32.2 us; the launch traced here: 32.1 us
  Pallas kernels  31.5 us (98%)
  between operations  0.64 us (2%)
    pallas_call x1, Pallas kernels, shards(): pl.pallas_call(functools.partial(kernel, sizes), out_shape=(whole, whole)...  30.1 us
    pallas_call x1, Pallas kernels, shards(): pl.pallas_call(leave, out_shape=(whole, whole), in_specs=[pl.BlockSpec(me...  1.33 us

profile of v3, /device:TPU:64, one launch (start us, length us, event | category | flops | bytes accessed | tf_op | source)
XLA Modules:
  0.0 32.1 jit_solution(4508311899087156785)
XLA Ops:
  0.6 30.1 %shard_map.122 = (f32[1,1,128,2048]{3,2,1,0:T(8,128)S(1)}, f32[1,1,128,2048]{3,2,1,0:T(8,128)S(1)}) custom-call(f32[1,1,128,2048]{3,2,1,0:T(8,128)} %initial.1, bf16[16,12,128,128]{3,2,1,0:T(8,128)(2,1)} %block_values.1, s32[16,12]{1,0:T(8,128)} %refs_0_.1, s32[2,12]{1,0:T(2,128)} %bitcast.1, f32[12]{0:T(128)} %refs_2_.1, s32[8]{0:T(128)} %refs_3_.1, ...), custom_call_target="tpu_custom_call" | custom-call | tf_op jit(solution)/shard_map/pallas_call | solution.py:352
  30.8 1.3 %shard_map.123 = (f32[1,1,128,2048]{3,2,1,0:T(8,128)}, f32[1,1,128,2048]{3,2,1,0:T(8,128)}) custom-call(f32[1,1,128,2048]{3,2,1,0:T(8,128)S(1)} %get-tuple-element.4.previous, f32[1,1,128,2048]{3,2,1,0:T(8,128)S(1)} %get-tuple-element.5.current), custom_call_target="tpu_custom_call" | custom-call | tf_op jit(solution)/shard_map/pallas_call | solution.py:380

commit v4 on v3

--- a/solution.py
+++ b/solution.py
@@ -157,14 +157,15 @@
         for k in range(CROSS):
             exchange(step, j, k).start()
 
-    for i in range(9):
+    load_small(7).start()
+    for j in range(chunks):
+        load(j).start()
+    others = [i for i in range(9) if i != 7]
+    for i in others:
         load_small(i).start()
     for j in range(chunks):
-        load(j).start()
-    for j in range(chunks):
         load_values(j).start()
-    for i in range(9):
-        load_small(i).wait()
+    load_small(7).wait()
 
     sites = [cross_sites[k] for k in range(CROSS)]
     column = lanes(columns)
@@ -183,6 +184,8 @@
         keep(0, j, states[1, j])
         send(0, j)
 
+    for i in others:
+        load_small(i).wait()
     crossing = [[], []]
     for pair in range(CROSS // 2):
         upper = lanes(columns) >= half

time: 32.2 us -> 32.2 us (level)
  no operation moved by 1% of the time
where the time goes in v4:
time: 32.2 us; the launch traced here: 32.1 us
  Pallas kernels  31.5 us (98%)
  between operations  0.64 us (2%)
    pallas_call x1, Pallas kernels, shards(): pl.pallas_call(functools.partial(kernel, sizes), out_shape=(whole, whole)...  30.1 us
    pallas_call x1, Pallas kernels, shards(): pl.pallas_call(leave, out_shape=(whole, whole), in_specs=[pl.BlockSpec(me...  1.33 us

profile of v4, /device:TPU:64, one launch (start us, length us, event | category | flops | bytes accessed | tf_op | source)
XLA Modules:
  0.0 32.1 jit_solution(11042322186021417833)
XLA Ops:
  0.6 30.1 %shard_map.122 = (f32[1,1,128,2048]{3,2,1,0:T(8,128)S(1)}, f32[1,1,128,2048]{3,2,1,0:T(8,128)S(1)}) custom-call(f32[1,1,128,2048]{3,2,1,0:T(8,128)} %initial.1, bf16[16,12,128,128]{3,2,1,0:T(8,128)(2,1)} %block_values.1, s32[16,12]{1,0:T(8,128)} %refs_0_.1, s32[2,12]{1,0:T(2,128)} %bitcast.1, f32[12]{0:T(128)} %refs_2_.1, s32[8]{0:T(128)} %refs_3_.1, ...), custom_call_target="tpu_custom_call" | custom-call | tf_op jit(solution)/shard_map/pallas_call | solution.py:355
  30.8 1.3 %shard_map.123 = (f32[1,1,128,2048]{3,2,1,0:T(8,128)}, f32[1,1,128,2048]{3,2,1,0:T(8,128)}) custom-call(f32[1,1,128,2048]{3,2,1,0:T(8,128)S(1)} %get-tuple-element.4.previous, f32[1,1,128,2048]{3,2,1,0:T(8,128)S(1)} %get-tuple-element.5.current), custom_call_target="tpu_custom_call" | custom-call | tf_op jit(solution)/shard_map/pallas_call | solution.py:383

commit v5 on v4

--- a/solution.py
+++ b/solution.py
@@ -305,6 +305,8 @@
         ahead[...] += own_product(step + 1, 0, rows - PARTS, PARTS, False)
 
     last = STEPS - 1
+    for step in range(last):
+        departure(step).wait()
 
     @pl.loop(0, chunks - 1)
     def _(j):
@@ -314,11 +316,9 @@
         ahead[...] = own_product(last, j + 1, 0, rows, True)
 
     store(previous_out, chunks - 1, states[STEPS, chunks - 1])
+    departure(last).wait()
     arrive(last, chunks - 1)
     store(current_out, chunks - 1, next_state(last, chunks - 1, 2.0))
-
-    for step in range(STEPS):
-        departure(step).wait()
 
 
 def leave(previous, current, previous_out, current_out, sem):

time: 32.2 us -> 32.2 us (level)
  no operation moved by 1% of the time
where the time goes in v5:
time: 32.2 us; the launch traced here: 32.1 us
  Pallas kernels  31.5 us (98%)
  between operations  0.64 us (2%)
    pallas_call x1, Pallas kernels, shards(): pl.pallas_call(functools.partial(kernel, sizes), out_shape=(whole, whole)...  30.1 us
    pallas_call x1, Pallas kernels, shards(): pl.pallas_call(leave, out_shape=(whole, whole), in_specs=[pl.BlockSpec(me...  1.33 us

profile of v5, /device:TPU:64, one launch (start us, length us, event | category | flops | bytes accessed | tf_op | source)
XLA Modules:
  0.0 32.1 jit_solution(14665416050529644030)
XLA Ops:
  0.6 30.1 %shard_map.122 = (f32[1,1,128,2048]{3,2,1,0:T(8,128)S(1)}, f32[1,1,128,2048]{3,2,1,0:T(8,128)S(1)}) custom-call(f32[1,1,128,2048]{3,2,1,0:T(8,128)} %initial.1, bf16[16,12,128,128]{3,2,1,0:T(8,128)(2,1)} %block_values.1, s32[16,12]{1,0:T(8,128)} %refs_0_.1, s32[2,12]{1,0:T(2,128)} %bitcast.1, f32[12]{0:T(128)} %refs_2_.1, s32[8]{0:T(128)} %refs_3_.1, ...), custom_call_target="tpu_custom_call" | custom-call | tf_op jit(solution)/shard_map/pallas_call | solution.py:355
  30.8 1.3 %shard_map.123 = (f32[1,1,128,2048]{3,2,1,0:T(8,128)}, f32[1,1,128,2048]{3,2,1,0:T(8,128)}) custom-call(f32[1,1,128,2048]{3,2,1,0:T(8,128)S(1)} %get-tuple-element.4.previous, f32[1,1,128,2048]{3,2,1,0:T(8,128)S(1)} %get-tuple-element.5.current), custom_call_target="tpu_custom_call" | custom-call | tf_op jit(solution)/shard_map/pallas_call | solution.py:383
